TPU v7x, 32 devices: a whole 2x2x4 slice. The times are simulated.
32 devices in a mesh: expert: 8 (over z, y), layer: 4 (over x, core).
Axes of the slice: x: 2, y: 2, z: 4, core: 2. Of those that a mesh axis runs over, the one named last changes fastest.
Arguments:
- gradient: bfloat16 [32, 16, 1536], P(('layer', 'expert')), parts along dimension 0, may hold values from -80 to 80
- prior_stat: float32 [32, 8], P('layer'), parts along dimension 0, may hold values from -600 to 600, as said below
Outputs:
- update: bfloat16 [32, 16, 1536], P(('layer', 'expert')), parts along dimension 0
- statistic: float32 [32, 8], P('layer'), parts along dimension 0
There are 4 independent parts, one for each index of `layer`. A program takes and returns all parts, laid end to end along the dimension named above; each array names one. Nothing has to cross between parts.
Inputs may be any that keep to these rules, and one draw needn't show every extreme that they name: `prior_stat`: symmetric positive definite.
All inputs are finite; a program needn't handle non-finite values.
Results may differ from a plain program's by a relative error of at most 0.001.
The roundings to bfloat16 on the way count: a program that leaves them out, or rounds other values in their place, can miss the bound.
Values may be sent and summed in bfloat16 or wider, within the bound.
A program may use at most 64 MiB of HBM per device.

v0:
```python
import jax
import jax.numpy as jnp
from jax import lax
from jax.sharding import PartitionSpec as P

ITERS = 5


ridge_rate = 0.001
energy_floor = 1e-06


def matmul_high(left, right):
    return jnp.dot(left, right, precision=lax.Precision.HIGHEST, preferred_element_type=jnp.float32)


def inverse_root(statistic):
    count_rows = statistic.shape[0]
    identity = jnp.eye(count_rows, dtype=jnp.float32)
    ridge_term = ridge_rate * jnp.trace(statistic) / count_rows
    shifted = statistic + ridge_term * identity
    start_scale = 2.5 / jnp.sqrt(jnp.sum(shifted * shifted))
    matrix = start_scale * shifted
    root = start_scale**0.25 * identity
    for repeat in range(ITERS):
        factor = 1.25 * identity - 0.25 * matrix
        root = matmul_high(root, factor)
        square = matmul_high(factor, factor)
        matrix = matmul_high(matmul_high(square, square), matrix)
    return root


def apply_graft(mixed_bf, graft):
    fenced = lax.optimization_barrier(mixed_bf)
    return (graft * fenced.astype(jnp.float32)).astype(jnp.bfloat16)


def slice_grams(pieces):
    grams = jnp.einsum("eqrf,gqrf->eqrg", pieces, pieces, preferred_element_type=jnp.float32)
    return (pieces, grams)


def body(gradient, prior_stat):
    experts = prior_stat.shape[0]
    owners = lax.axis_size("expert")
    local_experts = gradient.shape[0]
    slab_rows = gradient.shape[1]
    width = gradient.shape[2]
    entry_count = slab_rows * width
    slice_rows = slab_rows // owners
    blocked = gradient.reshape(local_experts, owners, slice_rows, width)
    regrouped, row_grams = slice_grams(
        lax.all_to_all(blocked, "expert", split_axis=1, concat_axis=0, tiled=True)
    )
    summed = lax.psum(jnp.sum(row_grams, axis=(1, 2)), "expert")
    gram_mean = summed / entry_count
    statistic = prior_stat + gram_mean
    root_bf = inverse_root(statistic).astype(jnp.bfloat16)
    flattened = regrouped.reshape(experts, -1)
    products = jnp.dot(root_bf, flattened, preferred_element_type=jnp.float32)
    mixed_bf = products.astype(jnp.bfloat16).reshape(experts, slice_rows, width)
    root_wide = root_bf.astype(jnp.float32)
    update_energy = jnp.sum(matmul_high(root_wide, gram_mean) * root_wide) / experts
    grad_energy = jnp.trace(gram_mean) / experts
    graft = jnp.sqrt((grad_energy + energy_floor) / (update_energy + energy_floor))
    grafted = apply_graft(mixed_bf, graft)
    update = lax.all_to_all(grafted, "expert", split_axis=0, concat_axis=1, tiled=True)
    return (update, statistic)


def solution(mesh):
    placed = (P(("layer", "expert"), None, None), P("layer", None))
    return jax.shard_map(
        body,
        mesh=mesh,
        in_specs=placed,
        out_specs=(P(("layer", "expert"), None, None), P("layer", None)),
        check_vma=False,
    )
```

profile of v0, /device:TPU:0, one launch (start us, length us, event | category | flops | bytes accessed | tf_op | source)
XLA Modules:
  0.0 50.7 jit_solution(7048645987614553434)
XLA Ops:
  0.6 0.8 %reshape.28 = bf16[1,8,2,1536]{3,2,1,0:T(2,128)(2,1)S(1)} reshape(bf16[1,16,1536]{2,1,0:T(8,128)(2,1)} %param.2) | data formatting | bytes 98304 | tf_op jit(solution)/shard_map/reshape | solution.py:51
  1.5 13.9 %all_to_all.21 = bf16[1,8,2,1536]{3,2,0,1:T(2,128)(2,1)S(1)} all-to-all(bf16[1,8,2,1536]{3,2,0,1:T(2,128)(2,1)S(1)} %bitcast.37), channel_id=1, replica_groups=mesh['expert'=8,'layer'=4] {'expert'}, dimensions={1} | all-to-all | bytes 98304 | tf_op jit(solution)/shard_map/all_to_all | solution.py:53
  15.4 0.1 convolution_bitcast_fusion
  15.5 0.0 copy-start.1
  15.5 18.0 %psum.7 = f32[8,8]{1,0:T(8,128)S(1)} all-reduce(f32[8,8]{1,0:T(8,128)S(1)} %convolution_bitcast_fusion), channel_id=1, replica_groups=mesh['expert'=8,'layer'=4] {'expert'}, use_global_device_ids=true, to_apply=%region_0.0 | all-reduce | flops 64 | bytes 512 | tf_op jit(solution)/shard_map/psum | solution.py:55
  33.5 0.0 copy-done.1
  33.5 0.7 %select_reduce_fusion = (f32[]{:T(128)}, f32[8,8]{1,0:T(8,128)S(1)}, f32[]{:T(128)}) fusion(f32[8,8]{1,0:T(8,128)S(1)} %copy-done.1, f32[8,8]{1,0:T(8,128)S(1)} %psum.7), kind=kLoop, calls=%fused_computation.18 | loop fusion | flops 446 | bytes 776 | tf_op jit(solution)/shard_map/jit(trace)/reduce_sum | solution.py:20
  34.2 0.0 copy-start
  34.8 0.6 %multiply_reduce_fusion = f32[]{:T(128)} fusion(f32[8,8]{1,0:T(8,128)S(1)} %get-tuple-element.3, f32[]{:T(128)S(6)} %div.24), kind=kLoop, calls=%fused_computation.16 | loop fusion | flops 319 | bytes 264 | tf_op jit(solution)/shard_map/reduce_sum | solution.py:22
  36.1 0.1 fusion.15
  36.3 0.1 fusion.4
  36.5 0.1 fusion.71
  36.6 0.0 copy-done
  36.6 0.1 fusion.6
  36.7 0.1 fusion.9
  36.9 0.1 fusion.10
  37.0 0.1 fusion.72
  37.1 0.1 fusion.73
  37.3 0.1 fusion.11
  37.4 0.1 fusion.12
  37.5 0.1 fusion.74
  37.7 0.1 fusion.75
  37.8 0.1 fusion.13
  38.0 0.1 fusion.14
  38.1 0.1 fusion.76
  38.2 0.1 fusion
  38.4 0.1 convolution_convert_fusion.1
  38.5 0.7 %fusion.1 = f32[]{:T(128)} fusion(bf16[8,8]{1,0:T(8,128)(2,1)S(1)} %convolution_convert_fusion.1, f32[8,8]{1,0:T(8,128)S(1)} %psum.7), kind=kOutput, calls=%fused_computation.6 | convolution fusion | flops 6399 | bytes 388 | tf_op jit(solution)/shard_map/dot_general | solution.py:14
  40.7 0.1 convolution_convert_fusion
  40.9 9.2 %all_to_all.22 = bf16[8,2,1536]{2,1,0:T(2,128)(2,1)S(1)} all-to-all(bf16[8,2,1536]{2,1,0:T(2,128)(2,1)S(1)} %copy.12), channel_id=1, replica_groups=mesh['expert'=8,'layer'=4] {'expert'}, dimensions={0} | all-to-all | bytes 98304 | tf_op jit(solution)/shard_map/all_to_all | solution.py:67
  50.1 0.6 %all_to_all.8 = bf16[1,16,1536]{2,1,0:T(8,128)(2,1)} reshape(bf16[8,2,1536]{2,1,0:T(2,128)(2,1)S(1)} %all_to_all.22) | data formatting | bytes 98304 | tf_op jit(solution)/shard_map/all_to_all | solution.py:67
  (3 shorter events, 0.1 us)
Async XLA Ops:
  15.5 18.0 %copy-start.1 = (f32[8,8]{1,0:T(8,128)S(1)}, f32[8,8]{1,0:T(8,128)}, u32[]{:S(2)}) copy-start(f32[8,8]{1,0:T(8,128)} %param.3) | copy-start | bytes 772
  34.2 2.4 %copy-start = (f32[8,8]{1,0:T(8,128)}, f32[8,8]{1,0:T(8,128)S(1)}, u32[]{:S(2)}) copy-start(f32[8,8]{1,0:T(8,128)S(1)} %get-tuple-element.3) | copy-start | bytes 772
where the time goes:
time: 51 us; the launch traced here: 50.7 us
  blocking collectives  41.1 us (81%)
  between operations  3.51 us (7%)
  matrix products  3.31 us (6%)
  local copies, waits for them, and re-layouts  1.52 us (3%)
  other arithmetic  1.3 us (3%)
    psum x1, blocking collectives, body(): summed = lax.psum(jnp.sum(row_grams, axis=(1, 2)), 'expert')  18 us
    all_to_all x1, blocking collectives, body(): lax.all_to_all(blocked, 'expert', split_axis=1, concat_axis=0, tiled=True)  13.9 us
    all_to_all x1, blocking collectives, body(): lax.all_to_all(grafted, 'expert', split_axis=0, concat_axis=1, tiled=True)  9.17 us
    dot_general x18, matrix products, matmul_high(): jnp.dot(left, right, precision=lax.Precision.HIGHEST, preferred_element_t...  3.05 us

commit v1 on v0

--- a/solution.py
+++ b/solution.py
@@ -1,13 +1,17 @@
+import functools
+
 import jax
 import jax.numpy as jnp
 from jax import lax
+from jax.experimental import pallas as pl
+from jax.experimental.pallas import tpu as pltpu
 from jax.sharding import PartitionSpec as P
 
 ITERS = 5
-
-
 ridge_rate = 0.001
 energy_floor = 1e-06
+LANES = 128
+VMEM_BUDGET = 16 * 1024 * 1024
 
 
 def matmul_high(left, right):
@@ -40,7 +44,7 @@
     return (pieces, grams)
 
 
-def body(gradient, prior_stat):
+def wide_body(gradient, prior_stat):
     experts = prior_stat.shape[0]
     owners = lax.axis_size("expert")
     local_experts = gradient.shape[0]
@@ -68,6 +72,167 @@
     return (update, statistic)
 
 
+def splat_rows(columns, keep):
+    for m, column in enumerate(columns):
+        keep[m] = column
+
+
+def entry(keep, k, m):
+    return jnp.broadcast_to(keep[m, k : k + 1, :], keep.shape[1:])
+
+
+def times(left, keep):
+    size = len(left)
+    out = []
+    for m in range(size):
+        terms = [left[k] * entry(keep, k, m) for k in range(size)]
+        while len(terms) > 1:
+            terms = [terms[i] + terms[i + 1] if i + 1 < len(terms) else terms[i] for i in range(0, len(terms), 2)]
+        out.append(terms[0])
+    return out
+
+
+def total(tiles):
+    acc = tiles[0]
+    for tile in tiles[1:]:
+        acc = acc + tile
+    return jnp.broadcast_to(jnp.sum(acc, axis=0, keepdims=True), acc.shape)
+
+
+def kernel(
+    owners, gradient_ref, prior_ref, update_ref, statistic_ref, held, keep_gram, keep_matrix, keep_factor, keep_square,
+    local_sem, send_sem, recv_sem,
+):
+    me = lax.axis_index("expert")
+    experts = owners
+    slab_rows, width = held.shape[1:]
+    rows = experts * slab_rows
+
+    local = pltpu.make_async_copy(gradient_ref.at[0], held.at[me], local_sem)
+    local.start()
+    barrier = pltpu.get_barrier_semaphore()
+    for step in range(1, owners):
+        peer = lax.rem(me + step, owners)
+        pl.semaphore_signal(barrier, inc=1, device_id={"expert": peer}, device_id_type=pl.DeviceIdType.MESH)
+    pl.semaphore_wait(barrier, owners - 1)
+    copies = []
+    for step in range(1, owners):
+        peer = lax.rem(me + step, owners)
+        copy = pltpu.make_async_remote_copy(
+            src_ref=gradient_ref.at[0],
+            dst_ref=held.at[me],
+            send_sem=send_sem.at[step],
+            recv_sem=recv_sem.at[step],
+            device_id={"expert": peer},
+            device_id_type=pl.DeviceIdType.MESH,
+        )
+        copy.start()
+        copies.append(copy)
+
+    tile = (experts, LANES)
+    row = lax.broadcasted_iota(jnp.int32, tile, 0)
+    lane = lax.broadcasted_iota(jnp.int32, tile, 1)
+    unit = [jnp.where(row == k, 1.0, 0.0).astype(jnp.float32) for k in range(experts)]
+    prior_wide = [jnp.broadcast_to(prior_ref[:, k : k + 1], tile) for k in range(experts)]
+
+    local.wait()
+    for copy in copies:
+        copy.wait()
+
+    flat = held[...].reshape(rows, width)
+    full = lax.dot_general(flat, flat, (((1,), (1,)), ((), ())), preferred_element_type=jnp.float32)
+    own = lax.broadcasted_iota(jnp.int32, (rows, rows), 0) % slab_rows
+    other = lax.broadcasted_iota(jnp.int32, (rows, rows), 1) % slab_rows
+    diagonal = jnp.where(own == other, full, 0.0)
+    paired = jnp.sum(diagonal.reshape(experts, slab_rows, rows), axis=1)
+    column_of = lax.broadcasted_iota(jnp.int32, (experts, rows), 1) // slab_rows
+    gram_mean = [
+        jnp.broadcast_to(
+            jnp.sum(jnp.where(column_of == k, paired, 0.0), axis=1, keepdims=True) / (slab_rows * width), tile
+        )
+        for k in range(experts)
+    ]
+    splat_rows(gram_mean, keep_gram)
+    statistic = [prior_wide[k] + gram_mean[k] for k in range(experts)]
+    shown = statistic[0]
+    for k in range(1, experts):
+        shown = jnp.where(lane == k, statistic[k], shown)
+    statistic_ref[...] = shown[:, :experts]
+
+    ridge_term = ridge_rate * total([unit[k] * statistic[k] for k in range(experts)]) / experts
+    shifted = [statistic[k] + ridge_term * unit[k] for k in range(experts)]
+    start_scale = 2.5 / jnp.sqrt(total([s * s for s in shifted]))
+    matrix = [start_scale * s for s in shifted]
+    start_root = jnp.sqrt(jnp.sqrt(start_scale))
+    root = [start_root * u for u in unit]
+    for repeat in range(ITERS):
+        factor = [1.25 * unit[k] - 0.25 * matrix[k] for k in range(experts)]
+        splat_rows(factor, keep_factor)
+        if repeat == 0:
+            root = [start_root * f for f in factor]
+        else:
+            root = times(root, keep_factor)
+        if repeat < ITERS - 1:
+            splat_rows(matrix, keep_matrix)
+            square = times(factor, keep_factor)
+            splat_rows(square, keep_square)
+            matrix = times(times(square, keep_square), keep_matrix)
+
+    root_wide = [r.astype(jnp.bfloat16).astype(jnp.float32) for r in root]
+    splat_rows(root_wide, keep_factor)
+    mine = [jnp.broadcast_to(keep_factor[g, pl.ds(me, 1), :], tile)[:1] for g in range(experts)]
+    spread = times(root_wide, keep_gram)
+    update_energy = total([spread[k] * root_wide[k] for k in range(experts)]) / experts
+    grad_energy = total([unit[k] * gram_mean[k] for k in range(experts)]) / experts
+    graft = jnp.sqrt((grad_energy + energy_floor) / (update_energy + energy_floor))[:1]
+    for start in range(0, width, LANES):
+        columns = slice(start, start + LANES)
+        products = mine[0] * held[0, :, columns].astype(jnp.float32)
+        for g in range(1, experts):
+            products = products + mine[g] * held[g, :, columns].astype(jnp.float32)
+        mixed = products.astype(jnp.bfloat16)
+        update_ref[0, :, columns] = (graft * mixed.astype(jnp.float32)).astype(jnp.bfloat16)
+
+
+def gathered_body(gradient, prior_stat):
+    owners = lax.axis_size("expert")
+    experts = prior_stat.shape[0]
+    slab_rows, width = gradient.shape[1:]
+    keep = pltpu.VMEM((experts, experts, LANES), jnp.float32)
+    return pl.pallas_call(
+        functools.partial(kernel, owners),
+        out_shape=(
+            jax.ShapeDtypeStruct(gradient.shape, jnp.bfloat16),
+            jax.ShapeDtypeStruct(prior_stat.shape, jnp.float32),
+        ),
+        in_specs=[pl.BlockSpec(memory_space=pl.ANY), pl.BlockSpec(memory_space=pltpu.VMEM)],
+        out_specs=(pl.BlockSpec(memory_space=pltpu.VMEM), pl.BlockSpec(memory_space=pltpu.VMEM)),
+        scratch_shapes=[
+            pltpu.VMEM((experts, slab_rows, width), jnp.bfloat16),
+            keep,
+            keep,
+            keep,
+            keep,
+            pltpu.SemaphoreType.DMA,
+            pltpu.SemaphoreType.DMA((owners,)),
+            pltpu.SemaphoreType.DMA((owners,)),
+        ],
+        compiler_params=pltpu.CompilerParams(collective_id=0, has_side_effects=True),
+        name="shampoo_step",
+    )(gradient, prior_stat)
+
+
+def body(gradient, prior_stat):
+    owners = lax.axis_size("expert")
+    experts = prior_stat.shape[0]
+    gathered_bytes = 2 * experts * gradient.shape[1] * gradient.shape[2]
+    fits = gathered_bytes <= VMEM_BUDGET and experts == owners and experts == 8
+    regular = gradient.shape[1] % 16 == 0 and gradient.shape[2] % LANES == 0
+    if fits and regular:
+        return gathered_body(gradient, prior_stat)
+    return wide_body(gradient, prior_stat)
+
+
 def solution(mesh):
     placed = (P(("layer", "expert"), None, None), P("layer", None))
     return jax.shard_map(

time: 51 us -> 18.5 us (0.36)
  the two profiles are of different devices: /device:TPU:0 before, /device:TPU:15 now
where the time goes in v1:
time: 18.5 us; the launch traced here: 18.3 us
  Pallas kernels  15.6 us (84%)
  local copies, waits for them, and re-layouts  2.02 us (11%)
  between operations  0.65 us (4%)
    pallas_call x1, Pallas kernels, gathered_body(): pl.pallas_call(functools.partial(kernel, owners), out_shape=(jax.ShapeDty...  15.6 us
    unnamed x4, local copies, waits for them, and re-layouts  2.02 us

profile of v1, /device:TPU:15, one launch (start us, length us, event | category | flops | bytes accessed | tf_op | source)
XLA Modules:
  0.0 18.3 jit_solution(16644830710974660354)
XLA Ops:
  0.6 15.6 %shampoo_step.1 = (bf16[1,16,1536]{2,1,0:T(8,128)(2,1)}, f32[8,8]{1,0:T(8,128)}) custom-call(bf16[1,16,1536]{2,1,0:T(8,128)(2,1)} %gradient_ref.1, f32[8,8]{1,0:T(8,128)} %prior_ref.1), custom_call_target="tpu_custom_call" | custom-call | tf_op jit(solution)/shard_map/shampoo_step/pallas_call | solution.py:202
  16.2 0.0 copy-start
  16.2 1.4 %copy.6 = bf16[1,16,1536]{2,1,0:T(8,128)(2,1)} copy(bf16[1,16,1536]{2,1,0:T(8,128)(2,1)} %get-tuple-element.4) | data formatting | bytes 98304
  17.7 0.0 copy-done
  17.7 0.6 %copy.7 = f32[8,8]{1,0:T(8,128)} copy(f32[8,8]{1,0:T(8,128)S(1)} %copy-done) | data formatting | bytes 512
Async XLA Ops:
  16.2 1.4 %copy-start = (f32[8,8]{1,0:T(8,128)S(1)}, f32[8,8]{1,0:T(8,128)}, u32[]{:S(2)}) copy-start(f32[8,8]{1,0:T(8,128)} %get-tuple-element.5) | copy-start | bytes 772

commit v2 on v1

--- a/solution.py
+++ b/solution.py
@@ -12,6 +12,10 @@
 energy_floor = 1e-06
 LANES = 128
 VMEM_BUDGET = 16 * 1024 * 1024
+KERNEL_VMEM = 32 * 1024 * 1024
+PAIR = 2
+RING = 4
+COPIES = 13
 
 
 def matmul_high(left, right):
@@ -100,44 +104,72 @@
 
 
 def kernel(
-    owners, gradient_ref, prior_ref, update_ref, statistic_ref, held, keep_gram, keep_matrix, keep_factor, keep_square,
-    local_sem, send_sem, recv_sem,
+    owners, gradient_ref, prior_hbm, mixed_ref, statistic_ref, graft_ref, held, keep_gram, keep_matrix, keep_factor,
+    keep_square, prior_ref, local_sem, prior_sem, send_sem, recv_sem,
 ):
     me = lax.axis_index("expert")
     experts = owners
     slab_rows, width = held.shape[1:]
     rows = experts * slab_rows
-
+    half = slab_rows // 2
+    ring = owners // PAIR
+    place, side = me // PAIR, me % PAIR
+
+    def at(step, flip):
+        return lax.rem(place + step + ring, ring) * PAIR + lax.rem(side + flip, PAIR)
+
+    peers = [(0, 1), (1, 0), (-1, 0), (1, 1), (-1, 1)]
+    barrier = pltpu.get_barrier_semaphore()
+    for step, flip in peers:
+        pl.semaphore_signal(
+            barrier, inc=1, device_id={"expert": at(step, flip)}, device_id_type=pl.DeviceIdType.MESH
+        )
     local = pltpu.make_async_copy(gradient_ref.at[0], held.at[me], local_sem)
     local.start()
-    barrier = pltpu.get_barrier_semaphore()
-    for step in range(1, owners):
-        peer = lax.rem(me + step, owners)
-        pl.semaphore_signal(barrier, inc=1, device_id={"expert": peer}, device_id_type=pl.DeviceIdType.MESH)
-    pl.semaphore_wait(barrier, owners - 1)
-    copies = []
-    for step in range(1, owners):
-        peer = lax.rem(me + step, owners)
+    prior_copy = pltpu.make_async_copy(prior_hbm, prior_ref, prior_sem)
+    prior_copy.start()
+    pl.semaphore_wait(barrier, len(peers))
+
+    made = []
+
+    def send(source, owner, part, step, flip):
+        span = slice(None) if part is None else pl.ds(part * half, half)
         copy = pltpu.make_async_remote_copy(
-            src_ref=gradient_ref.at[0],
-            dst_ref=held.at[me],
-            send_sem=send_sem.at[step],
-            recv_sem=recv_sem.at[step],
-            device_id={"expert": peer},
+            src_ref=source.at[span],
+            dst_ref=held.at[owner, span],
+            send_sem=send_sem.at[len(made)],
+            recv_sem=recv_sem.at[len(made)],
+            device_id={"expert": at(step, flip)},
             device_id_type=pl.DeviceIdType.MESH,
         )
         copy.start()
-        copies.append(copy)
+        made.append(copy)
+        return copy
+
+    own = gradient_ref.at[0]
+    first = [send(own, me, 0 if step > 0 else 1, step, flip) for flip in (0, 1) for step in (1, -1)]
+    rest = [send(own, me, None, 0, 1)]
+    rest += [send(own, me, 1 if step > 0 else 0, step, flip) for flip in (0, 1) for step in (1, -1)]
+    index = 0
+    for flip in (0, 1):
+        for step in (1, -1):
+            first[index].wait_recv()
+            owner = at(-step, flip)
+            rest.append(send(held.at[owner], owner, 0 if step > 0 else 1, step, 0))
+            index += 1
 
     tile = (experts, LANES)
     row = lax.broadcasted_iota(jnp.int32, tile, 0)
     lane = lax.broadcasted_iota(jnp.int32, tile, 1)
     unit = [jnp.where(row == k, 1.0, 0.0).astype(jnp.float32) for k in range(experts)]
+    prior_copy.wait()
     prior_wide = [jnp.broadcast_to(prior_ref[:, k : k + 1], tile) for k in range(experts)]
 
     local.wait()
-    for copy in copies:
-        copy.wait()
+    for copy in rest:
+        copy.wait_recv()
+    for copy in made:
+        copy.wait_send()
 
     flat = held[...].reshape(rows, width)
     full = lax.dot_general(flat, flat, (((1,), (1,)), ((), ())), preferred_element_type=jnp.float32)
@@ -157,7 +189,7 @@
     shown = statistic[0]
     for k in range(1, experts):
         shown = jnp.where(lane == k, statistic[k], shown)
-    statistic_ref[...] = shown[:, :experts]
+    statistic_ref[...] = shown
 
     ridge_term = ridge_rate * total([unit[k] * statistic[k] for k in range(experts)]) / experts
     shifted = [statistic[k] + ridge_term * unit[k] for k in range(experts)]
@@ -184,14 +216,23 @@
     spread = times(root_wide, keep_gram)
     update_energy = total([spread[k] * root_wide[k] for k in range(experts)]) / experts
     grad_energy = total([unit[k] * gram_mean[k] for k in range(experts)]) / experts
-    graft = jnp.sqrt((grad_energy + energy_floor) / (update_energy + energy_floor))[:1]
+    graft = jnp.sqrt((grad_energy + energy_floor) / (update_energy + energy_floor))
+    graft_ref[...] = graft
     for start in range(0, width, LANES):
         columns = slice(start, start + LANES)
         products = mine[0] * held[0, :, columns].astype(jnp.float32)
         for g in range(1, experts):
             products = products + mine[g] * held[g, :, columns].astype(jnp.float32)
-        mixed = products.astype(jnp.bfloat16)
-        update_ref[0, :, columns] = (graft * mixed.astype(jnp.float32)).astype(jnp.bfloat16)
+        mixed_ref[:, columns] = products.astype(jnp.bfloat16)
+
+
+def finish(mixed_ref, wide_ref, graft_ref, update_ref, statistic_ref):
+    graft = graft_ref[:1]
+    for start in range(0, mixed_ref.shape[1], LANES):
+        columns = slice(start, start + LANES)
+        mixed = mixed_ref[:, columns].astype(jnp.float32)
+        update_ref[0, :, columns] = (graft * mixed).astype(jnp.bfloat16)
+    statistic_ref[...] = wide_ref[:, : statistic_ref.shape[1]]
 
 
 def gathered_body(gradient, prior_stat):
@@ -199,34 +240,51 @@
     experts = prior_stat.shape[0]
     slab_rows, width = gradient.shape[1:]
     keep = pltpu.VMEM((experts, experts, LANES), jnp.float32)
-    return pl.pallas_call(
+    vmem = pl.BlockSpec(memory_space=pltpu.VMEM)
+    mixed, wide, graft = pl.pallas_call(
         functools.partial(kernel, owners),
         out_shape=(
-            jax.ShapeDtypeStruct(gradient.shape, jnp.bfloat16),
-            jax.ShapeDtypeStruct(prior_stat.shape, jnp.float32),
+            pltpu.VMEM((slab_rows, width), jnp.bfloat16),
+            pltpu.VMEM((experts, LANES), jnp.float32),
+            pltpu.VMEM((experts, LANES), jnp.float32),
         ),
-        in_specs=[pl.BlockSpec(memory_space=pl.ANY), pl.BlockSpec(memory_space=pltpu.VMEM)],
-        out_specs=(pl.BlockSpec(memory_space=pltpu.VMEM), pl.BlockSpec(memory_space=pltpu.VMEM)),
+        in_specs=[pl.BlockSpec(memory_space=pltpu.HBM)] * 2,
+        out_specs=(vmem, vmem, vmem),
         scratch_shapes=[
             pltpu.VMEM((experts, slab_rows, width), jnp.bfloat16),
             keep,
             keep,
             keep,
             keep,
+            pltpu.VMEM(prior_stat.shape, jnp.float32),
             pltpu.SemaphoreType.DMA,
-            pltpu.SemaphoreType.DMA((owners,)),
-            pltpu.SemaphoreType.DMA((owners,)),
+            pltpu.SemaphoreType.DMA,
+            pltpu.SemaphoreType.DMA((COPIES,)),
+            pltpu.SemaphoreType.DMA((COPIES,)),
         ],
-        compiler_params=pltpu.CompilerParams(collective_id=0, has_side_effects=True),
+        compiler_params=pltpu.CompilerParams(
+            collective_id=0, has_side_effects=True, vmem_limit_bytes=KERNEL_VMEM
+        ),
         name="shampoo_step",
     )(gradient, prior_stat)
+    return pl.pallas_call(
+        finish,
+        out_shape=(
+            jax.ShapeDtypeStruct(gradient.shape, jnp.bfloat16),
+            jax.ShapeDtypeStruct(prior_stat.shape, jnp.float32),
+        ),
+        in_specs=[vmem, vmem, vmem],
+        out_specs=(vmem, vmem),
+        compiler_params=pltpu.CompilerParams(vmem_limit_bytes=KERNEL_VMEM),
+        name="finish",
+    )(mixed, wide, graft)
 
 
 def body(gradient, prior_stat):
     owners = lax.axis_size("expert")
     experts = prior_stat.shape[0]
     gathered_bytes = 2 * experts * gradient.shape[1] * gradient.shape[2]
-    fits = gathered_bytes <= VMEM_BUDGET and experts == owners and experts == 8
+    fits = gathered_bytes <= VMEM_BUDGET and experts == owners and owners == PAIR * RING
     regular = gradient.shape[1] % 16 == 0 and gradient.shape[2] % LANES == 0
     if fits and regular:
         return gathered_body(gradient, prior_stat)

time: 18.5 us -> 18.6 us (level)
  the two profiles are of different devices: /device:TPU:15 before, /device:TPU:0 now
where the time goes in v2:
time: 18.6 us; the launch traced here: 18.4 us
  Pallas kernels  16.2 us (87%)
  local copies, waits for them, and re-layouts  1.48 us (8%)
  between operations  0.65 us (3%)
    pallas_call x1, Pallas kernels, gathered_body(): pl.pallas_call(functools.partial(kernel, owners), out_shape=(pltpu.VMEM((...  15.6 us
    unnamed x4, local copies, waits for them, and re-layouts  1.48 us
    pallas_call x1, Pallas kernels, gathered_body(): pl.pallas_call(finish, out_shape=(jax.ShapeDtypeStruct(gradient.shape, jn...  0.64 us

profile of v2, /device:TPU:0, one launch (start us, length us, event | category | flops | bytes accessed | tf_op | source)
XLA Modules:
  0.0 18.4 jit_solution(163260769532937167)
XLA Ops:
  0.6 0.0 copy-start
  0.6 0.8 %copy-done = bf16[1,16,1536]{2,1,0:T(8,128)(2,1)S(1)} copy-done((bf16[1,16,1536]{2,1,0:T(8,128)(2,1)S(1)}, bf16[1,16,1536]{2,1,0:T(8,128)(2,1)}, u32[]{:S(2)}) %copy-start) | copy-done | bytes 49176
  1.4 0.0 copy-start.1
  1.4 0.7 %copy-done.1 = f32[8,8]{1,0:T(8,128)S(1)} copy-done((f32[8,8]{1,0:T(8,128)S(1)}, f32[8,8]{1,0:T(8,128)}, u32[]{:S(2)}) %copy-start.1) | copy-done | bytes 280
  2.1 15.6 %shampoo_step.1 = (bf16[16,1536]{1,0:T(8,128)(2,1)S(1)}, f32[8,128]{1,0:T(8,128)S(1)}, f32[8,128]{1,0:T(8,128)S(1)}) custom-call(bf16[1,16,1536]{2,1,0:T(8,128)(2,1)S(1)} %copy-done, f32[8,8]{1,0:T(8,128)S(1)} %copy-done.1), custom_call_target="tpu_custom_call" | custom-call | tf_op jit(solution)/shard_map/shampoo_step/pallas_call | solution.py:244
  17.7 0.6 %finish.1 = (bf16[1,16,1536]{2,1,0:T(8,128)(2,1)}, f32[8,8]{1,0:T(8,128)}) custom-call(bf16[16,1536]{1,0:T(8,128)(2,1)S(1)} %get-tuple-element.5.mixed_ref, f32[8,128]{1,0:T(8,128)S(1)} %get-tuple-element.6.wide_ref, f32[8,128]{1,0:T(8,128)S(1)} %get-tuple-element.7.graft_ref), custom_call_target="tpu_custom_call" | custom-call | tf_op jit(solution)/shard_map/finish/pallas_call | solution.py:270
Async XLA Ops:
  0.6 0.8 %copy-start = (bf16[1,16,1536]{2,1,0:T(8,128)(2,1)S(1)}, bf16[1,16,1536]{2,1,0:T(8,128)(2,1)}, u32[]{:S(2)}) copy-start(bf16[1,16,1536]{2,1,0:T(8,128)(2,1)} %gradient_ref.1) | copy-start | bytes 147460
  1.4 0.7 %copy-start.1 = (f32[8,8]{1,0:T(8,128)S(1)}, f32[8,8]{1,0:T(8,128)}, u32[]{:S(2)}) copy-start(f32[8,8]{1,0:T(8,128)} %prior_hbm.1) | copy-start | bytes 772

commit v3 on v2

--- a/solution.py
+++ b/solution.py
@@ -14,8 +14,6 @@
 VMEM_BUDGET = 16 * 1024 * 1024
 KERNEL_VMEM = 32 * 1024 * 1024
 PAIR = 2
-RING = 4
-COPIES = 13
 
 
 def matmul_high(left, right):
@@ -105,58 +103,113 @@
 
 def kernel(
     owners, gradient_ref, prior_hbm, mixed_ref, statistic_ref, graft_ref, held, keep_gram, keep_matrix, keep_factor,
-    keep_square, prior_ref, local_sem, prior_sem, send_sem, recv_sem,
+    keep_square, prior_ref, local_sem, prior_sem, send_sem, recv_sem, up_ready, cross_ready,
 ):
     me = lax.axis_index("expert")
     experts = owners
     slab_rows, width = held.shape[1:]
     rows = experts * slab_rows
-    half = slab_rows // 2
-    ring = owners // PAIR
+    line = owners // PAIR
+    last = line - 1
     place, side = me // PAIR, me % PAIR
-
-    def at(step, flip):
-        return lax.rem(place + step + ring, ring) * PAIR + lax.rem(side + flip, PAIR)
-
-    peers = [(0, 1), (1, 0), (-1, 0), (1, 1), (-1, 1)]
+    partner = place * PAIR + 1 - side
+    opposite = (last - place) * PAIR + 1 - side
+
+    def here(position):
+        return position * PAIR + side
+
+    def signal(semaphore, device):
+        pl.semaphore_signal(semaphore, inc=1, device_id={"expert": device}, device_id_type=pl.DeviceIdType.MESH)
+
+    def copy(source, owner, sem, device):
+        return pltpu.make_async_remote_copy(
+            src_ref=source,
+            dst_ref=held.at[owner],
+            send_sem=send_sem.at[sem],
+            recv_sem=recv_sem.at[owner],
+            device_id={"expert": device},
+            device_id_type=pl.DeviceIdType.MESH,
+        )
+
+    CROSS, UP, DOWN, FAR = 0, line, 2 * line, 3 * line
+    own = gradient_ref.at[0]
+
     barrier = pltpu.get_barrier_semaphore()
-    for step, flip in peers:
-        pl.semaphore_signal(
-            barrier, inc=1, device_id={"expert": at(step, flip)}, device_id_type=pl.DeviceIdType.MESH
-        )
-    local = pltpu.make_async_copy(gradient_ref.at[0], held.at[me], local_sem)
+
+    @pl.when(side == 0)
+    def _():
+        signal(barrier, partner)
+
+    @pl.when(place == 0)
+    def _():
+        signal(barrier, opposite)
+
+    for position in range(1, line):
+
+        @pl.when(position > place)
+        def _():
+            signal(barrier, here(position))
+
+    local = pltpu.make_async_copy(own, held.at[me], local_sem)
     local.start()
     prior_copy = pltpu.make_async_copy(prior_hbm, prior_ref, prior_sem)
     prior_copy.start()
-    pl.semaphore_wait(barrier, len(peers))
-
-    made = []
-
-    def send(source, owner, part, step, flip):
-        span = slice(None) if part is None else pl.ds(part * half, half)
-        copy = pltpu.make_async_remote_copy(
-            src_ref=source.at[span],
-            dst_ref=held.at[owner, span],
-            send_sem=send_sem.at[len(made)],
-            recv_sem=recv_sem.at[len(made)],
-            device_id={"expert": at(step, flip)},
-            device_id_type=pl.DeviceIdType.MESH,
-        )
-        copy.start()
-        made.append(copy)
-        return copy
-
-    own = gradient_ref.at[0]
-    first = [send(own, me, 0 if step > 0 else 1, step, flip) for flip in (0, 1) for step in (1, -1)]
-    rest = [send(own, me, None, 0, 1)]
-    rest += [send(own, me, 1 if step > 0 else 0, step, flip) for flip in (0, 1) for step in (1, -1)]
-    index = 0
-    for flip in (0, 1):
-        for step in (1, -1):
-            first[index].wait_recv()
-            owner = at(-step, flip)
-            rest.append(send(held.at[owner], owner, 0 if step > 0 else 1, step, 0))
-            index += 1
+    greeted = place + side + place // last
+
+    @pl.when(greeted > 0)
+    def _():
+        pl.semaphore_wait(barrier, greeted)
+
+    @pl.when(place == last)
+    def _():
+        copy(own, me, FAR, opposite).start()
+
+    for position in range(last):
+
+        @pl.when(position < place)
+        def _():
+            copy(own, me, DOWN + position, here(position)).start()
+
+    @pl.when(place > 0)
+    def _():
+        signal(up_ready, here(place - 1))
+
+    @pl.when(side == 1)
+    def _():
+        signal(cross_ready, partner)
+
+    @pl.when(side == 0)
+    def _():
+        pl.semaphore_wait(cross_ready, 1)
+
+    copy(own, me, CROSS + place, partner).start()
+
+    @pl.when(place < last)
+    def _():
+        pl.semaphore_wait(up_ready, 1)
+        copy(own, me, UP + place, here(place + 1)).start()
+
+    for distance in range(1, line):
+
+        @pl.when(place + distance <= last)
+        def _():
+            position = place + distance
+            block = here(position)
+            copy(own, block, CROSS, partner).wait_recv()
+
+            if distance < last:
+                copy(held.at[block], block, CROSS + position, partner).start()
+
+        @pl.when(place - distance >= 0)
+        def _():
+            position = place - distance
+            block = here(position)
+            copy(own, block, CROSS, partner).wait_recv()
+            copy(held.at[block], block, CROSS + position, partner).start()
+
+            @pl.when(place < last)
+            def _():
+                copy(held.at[block], block, UP + position, here(place + 1)).start()
 
     tile = (experts, LANES)
     row = lax.broadcasted_iota(jnp.int32, tile, 0)
@@ -166,16 +219,14 @@
     prior_wide = [jnp.broadcast_to(prior_ref[:, k : k + 1], tile) for k in range(experts)]
 
     local.wait()
-    for copy in rest:
-        copy.wait_recv()
-    for copy in made:
-        copy.wait_send()
+    for position in range(line):
+        copy(own, position * PAIR + 1 - side, CROSS, partner).wait_recv()
 
     flat = held[...].reshape(rows, width)
     full = lax.dot_general(flat, flat, (((1,), (1,)), ((), ())), preferred_element_type=jnp.float32)
-    own = lax.broadcasted_iota(jnp.int32, (rows, rows), 0) % slab_rows
-    other = lax.broadcasted_iota(jnp.int32, (rows, rows), 1) % slab_rows
-    diagonal = jnp.where(own == other, full, 0.0)
+    left_row = lax.broadcasted_iota(jnp.int32, (rows, rows), 0) % slab_rows
+    right_row = lax.broadcasted_iota(jnp.int32, (rows, rows), 1) % slab_rows
+    diagonal = jnp.where(left_row == right_row, full, 0.0)
     paired = jnp.sum(diagonal.reshape(experts, slab_rows, rows), axis=1)
     column_of = lax.broadcasted_iota(jnp.int32, (experts, rows), 1) // slab_rows
     gram_mean = [
@@ -224,6 +275,24 @@
         for g in range(1, experts):
             products = products + mine[g] * held[g, :, columns].astype(jnp.float32)
         mixed_ref[:, columns] = products.astype(jnp.bfloat16)
+
+    for position in range(line):
+
+        @pl.when((place > 0) | (position < last))
+        def _():
+            copy(own, me, CROSS + position, partner).wait_send()
+
+        @pl.when((position <= place) & (place < last))
+        def _():
+            copy(own, me, UP + position, partner).wait_send()
+
+        @pl.when(position < place)
+        def _():
+            copy(own, me, DOWN + position, partner).wait_send()
+
+    @pl.when(place == last)
+    def _():
+        copy(own, me, FAR, partner).wait_send()
 
 
 def finish(mixed_ref, wide_ref, graft_ref, update_ref, statistic_ref):
@@ -259,14 +328,16 @@
             pltpu.VMEM(prior_stat.shape, jnp.float32),
             pltpu.SemaphoreType.DMA,
             pltpu.SemaphoreType.DMA,
-            pltpu.SemaphoreType.DMA((COPIES,)),
-            pltpu.SemaphoreType.DMA((COPIES,)),
+            pltpu.SemaphoreType.DMA((3 * owners // PAIR + 1,)),
+            pltpu.SemaphoreType.DMA((owners,)),
+            pltpu.SemaphoreType.REGULAR,
+            pltpu.SemaphoreType.REGULAR,
         ],
         compiler_params=pltpu.CompilerParams(
             collective_id=0, has_side_effects=True, vmem_limit_bytes=KERNEL_VMEM
         ),
         name="shampoo_step",
-    )(gradient, prior_stat)
+    )(*[pltpu.with_memory_space_constraint(x, pltpu.HBM) for x in (gradient, prior_stat)])
     return pl.pallas_call(
         finish,
         out_shape=(
@@ -284,7 +355,7 @@
     owners = lax.axis_size("expert")
     experts = prior_stat.shape[0]
     gathered_bytes = 2 * experts * gradient.shape[1] * gradient.shape[2]
-    fits = gathered_bytes <= VMEM_BUDGET and experts == owners and owners == PAIR * RING
+    fits = gathered_bytes <= VMEM_BUDGET and experts == owners and owners % PAIR == 0 and 2 * PAIR <= owners <= 8
     regular = gradient.shape[1] % 16 == 0 and gradient.shape[2] % LANES == 0
     if fits and regular:
         return gathered_body(gradient, prior_stat)

time: 18.6 us -> 19.1 us (1.027)
  the two profiles are of different devices: /device:TPU:0 before, /device:TPU:24 now
where the time goes in v3:
time: 19.1 us; the launch traced here: 18.9 us
  Pallas kernels  18.3 us (96%)
  between operations  0.64 us (3%)
    pallas_call x1, Pallas kernels, gathered_body(): pl.pallas_call(functools.partial(kernel, owners), out_shape=(pltpu.VMEM((...  17.6 us
    pallas_call x1, Pallas kernels, gathered_body(): pl.pallas_call(finish, out_shape=(jax.ShapeDtypeStruct(gradient.shape, jn...  0.64 us

profile of v3, /device:TPU:24, one launch (start us, length us, event | category | flops | bytes accessed | tf_op | source)
XLA Modules:
  0.0 18.9 jit_solution(16689339992685028987)
XLA Ops:
  0.6 17.6 %shampoo_step.1 = (bf16[16,1536]{1,0:T(8,128)(2,1)S(1)}, f32[8,128]{1,0:T(8,128)S(1)}, f32[8,128]{1,0:T(8,128)S(1)}) custom-call(bf16[1,16,1536]{2,1,0:T(8,128)(2,1)} %gradient_ref.1, f32[8,8]{1,0:T(8,128)} %prior_hbm.1), custom_call_target="tpu_custom_call" | custom-call | tf_op jit(solution)/shard_map/shampoo_step/pallas_call | solution.py:313
  18.3 0.6 %finish.1 = (bf16[1,16,1536]{2,1,0:T(8,128)(2,1)}, f32[8,8]{1,0:T(8,128)}) custom-call(bf16[16,1536]{1,0:T(8,128)(2,1)S(1)} %get-tuple-element.5.mixed_ref, f32[8,128]{1,0:T(8,128)S(1)} %get-tuple-element.6.wide_ref, f32[8,128]{1,0:T(8,128)S(1)} %get-tuple-element.7.graft_ref), custom_call_target="tpu_custom_call" | custom-call | tf_op jit(solution)/shard_map/finish/pallas_call | solution.py:341

commit v4 on v2

--- a/solution.py
+++ b/solution.py
@@ -266,7 +266,7 @@
             collective_id=0, has_side_effects=True, vmem_limit_bytes=KERNEL_VMEM
         ),
         name="shampoo_step",
-    )(gradient, prior_stat)
+    )(*[pltpu.with_memory_space_constraint(x, pltpu.HBM) for x in (gradient, prior_stat)])
     return pl.pallas_call(
         finish,
         out_shape=(

time: 18.6 us -> 17.3 us (0.930)
  local copies, waits for them, and re-layouts: 1.48 us -> 0 us
  Pallas kernels: 16.2 us -> 16.5 us
    unnamed x4 -> x0, local copies, waits for them, and re-layouts: 1.48 us -> none
    pallas_call x1, Pallas kernels: 15.6 us -> 15.9 us  [gathered_body(): pl.pallas_call(functools.partial(kernel, owners), out_shape=(pltpu.VMEM((...]
where the time goes in v4:
time: 17.3 us; the launch traced here: 17.1 us
  Pallas kernels  16.5 us (95%)
  between operations  0.64 us (4%)
    pallas_call x1, Pallas kernels, gathered_body(): pl.pallas_call(functools.partial(kernel, owners), out_shape=(pltpu.VMEM((...  15.9 us
    pallas_call x1, Pallas kernels, gathered_body(): pl.pallas_call(finish, out_shape=(jax.ShapeDtypeStruct(gradient.shape, jn...  0.64 us

profile of v4, /device:TPU:0, one launch (start us, length us, event | category | flops | bytes accessed | tf_op | source)
XLA Modules:
  0.0 17.1 jit_solution(3977713621007714286)
XLA Ops:
  0.6 15.9 %shampoo_step.1 = (bf16[16,1536]{1,0:T(8,128)(2,1)S(1)}, f32[8,128]{1,0:T(8,128)S(1)}, f32[8,128]{1,0:T(8,128)S(1)}) custom-call(bf16[1,16,1536]{2,1,0:T(8,128)(2,1)} %gradient_ref.1, f32[8,8]{1,0:T(8,128)} %prior_hbm.1), custom_call_target="tpu_custom_call" | custom-call | tf_op jit(solution)/shard_map/shampoo_step/pallas_call | solution.py:244
  16.5 0.6 %finish.1 = (bf16[1,16,1536]{2,1,0:T(8,128)(2,1)}, f32[8,8]{1,0:T(8,128)}) custom-call(bf16[16,1536]{1,0:T(8,128)(2,1)S(1)} %get-tuple-element.5.mixed_ref, f32[8,128]{1,0:T(8,128)S(1)} %get-tuple-element.6.wide_ref, f32[8,128]{1,0:T(8,128)S(1)} %get-tuple-element.7.graft_ref), custom_call_target="tpu_custom_call" | custom-call | tf_op jit(solution)/shard_map/finish/pallas_call | solution.py:270

commit v5 on v4

--- a/solution.py
+++ b/solution.py
@@ -13,9 +13,6 @@
 LANES = 128
 VMEM_BUDGET = 16 * 1024 * 1024
 KERNEL_VMEM = 32 * 1024 * 1024
-PAIR = 2
-RING = 4
-COPIES = 13
 
 
 def matmul_high(left, right):
@@ -111,52 +108,28 @@
     experts = owners
     slab_rows, width = held.shape[1:]
     rows = experts * slab_rows
-    half = slab_rows // 2
-    ring = owners // PAIR
-    place, side = me // PAIR, me % PAIR
-
-    def at(step, flip):
-        return lax.rem(place + step + ring, ring) * PAIR + lax.rem(side + flip, PAIR)
-
-    peers = [(0, 1), (1, 0), (-1, 0), (1, 1), (-1, 1)]
     barrier = pltpu.get_barrier_semaphore()
-    for step, flip in peers:
+    for step in range(1, owners):
         pl.semaphore_signal(
-            barrier, inc=1, device_id={"expert": at(step, flip)}, device_id_type=pl.DeviceIdType.MESH
+            barrier, inc=1, device_id={"expert": lax.rem(me + step, owners)}, device_id_type=pl.DeviceIdType.MESH
         )
     local = pltpu.make_async_copy(gradient_ref.at[0], held.at[me], local_sem)
     local.start()
     prior_copy = pltpu.make_async_copy(prior_hbm, prior_ref, prior_sem)
     prior_copy.start()
-    pl.semaphore_wait(barrier, len(peers))
-
+    pl.semaphore_wait(barrier, owners - 1)
     made = []
-
-    def send(source, owner, part, step, flip):
-        span = slice(None) if part is None else pl.ds(part * half, half)
+    for step in range(1, owners):
         copy = pltpu.make_async_remote_copy(
-            src_ref=source.at[span],
-            dst_ref=held.at[owner, span],
-            send_sem=send_sem.at[len(made)],
-            recv_sem=recv_sem.at[len(made)],
-            device_id={"expert": at(step, flip)},
+            src_ref=gradient_ref.at[0],
+            dst_ref=held.at[me],
+            send_sem=send_sem.at[step],
+            recv_sem=recv_sem.at[step],
+            device_id={"expert": lax.rem(me + step, owners)},
             device_id_type=pl.DeviceIdType.MESH,
         )
         copy.start()
         made.append(copy)
-        return copy
-
-    own = gradient_ref.at[0]
-    first = [send(own, me, 0 if step > 0 else 1, step, flip) for flip in (0, 1) for step in (1, -1)]
-    rest = [send(own, me, None, 0, 1)]
-    rest += [send(own, me, 1 if step > 0 else 0, step, flip) for flip in (0, 1) for step in (1, -1)]
-    index = 0
-    for flip in (0, 1):
-        for step in (1, -1):
-            first[index].wait_recv()
-            owner = at(-step, flip)
-            rest.append(send(held.at[owner], owner, 0 if step > 0 else 1, step, 0))
-            index += 1
 
     tile = (experts, LANES)
     row = lax.broadcasted_iota(jnp.int32, tile, 0)
@@ -166,10 +139,8 @@
     prior_wide = [jnp.broadcast_to(prior_ref[:, k : k + 1], tile) for k in range(experts)]
 
     local.wait()
-    for copy in rest:
-        copy.wait_recv()
     for copy in made:
-        copy.wait_send()
+        copy.wait()
 
     flat = held[...].reshape(rows, width)
     full = lax.dot_general(flat, flat, (((1,), (1,)), ((), ())), preferred_element_type=jnp.float32)
@@ -259,8 +230,8 @@
             pltpu.VMEM(prior_stat.shape, jnp.float32),
             pltpu.SemaphoreType.DMA,
             pltpu.SemaphoreType.DMA,
-            pltpu.SemaphoreType.DMA((COPIES,)),
-            pltpu.SemaphoreType.DMA((COPIES,)),
+            pltpu.SemaphoreType.DMA((owners,)),
+            pltpu.SemaphoreType.DMA((owners,)),
         ],
         compiler_params=pltpu.CompilerParams(
             collective_id=0, has_side_effects=True, vmem_limit_bytes=KERNEL_VMEM
@@ -284,7 +255,7 @@
     owners = lax.axis_size("expert")
     experts = prior_stat.shape[0]
     gathered_bytes = 2 * experts * gradient.shape[1] * gradient.shape[2]
-    fits = gathered_bytes <= VMEM_BUDGET and experts == owners and owners == PAIR * RING
+    fits = gathered_bytes <= VMEM_BUDGET and experts == owners and owners == 8
     regular = gradient.shape[1] % 16 == 0 and gradient.shape[2] % LANES == 0
     if fits and regular:
         return gathered_body(gradient, prior_stat)

time: 17.3 us -> 15.7 us (0.908)
  the two profiles are of different devices: /device:TPU:0 before, /device:TPU:13 now
where the time goes in v5:
time: 15.7 us; the launch traced here: 15.6 us
  Pallas kernels  15 us (96%)
  between operations  0.64 us (4%)
    pallas_call x1, Pallas kernels, gathered_body(): pl.pallas_call(functools.partial(kernel, owners), out_shape=(pltpu.VMEM((...  14.3 us
    pallas_call x1, Pallas kernels, gathered_body(): pl.pallas_call(finish, out_shape=(jax.ShapeDtypeStruct(gradient.shape, jn...  0.64 us

profile of v5, /device:TPU:13, one launch (start us, length us, event | category | flops | bytes accessed | tf_op | source)
XLA Modules:
  0.0 15.6 jit_solution(10229563965609934873)
XLA Ops:
  0.6 14.3 %shampoo_step.1 = (bf16[16,1536]{1,0:T(8,128)(2,1)S(1)}, f32[8,128]{1,0:T(8,128)S(1)}, f32[8,128]{1,0:T(8,128)S(1)}) custom-call(bf16[1,16,1536]{2,1,0:T(8,128)(2,1)} %gradient_ref.1, f32[8,8]{1,0:T(8,128)} %prior_hbm.1), custom_call_target="tpu_custom_call" | custom-call | tf_op jit(solution)/shard_map/shampoo_step/pallas_call | solution.py:215
  15.0 0.6 %finish.1 = (bf16[1,16,1536]{2,1,0:T(8,128)(2,1)}, f32[8,8]{1,0:T(8,128)}) custom-call(bf16[16,1536]{1,0:T(8,128)(2,1)S(1)} %get-tuple-element.5.mixed_ref, f32[8,128]{1,0:T(8,128)S(1)} %get-tuple-element.6.wide_ref, f32[8,128]{1,0:T(8,128)S(1)} %get-tuple-element.7.graft_ref), custom_call_target="tpu_custom_call" | custom-call | tf_op jit(solution)/shard_map/finish/pallas_call | solution.py:241

commit v6 on v5

--- a/solution.py
+++ b/solution.py
@@ -102,34 +102,55 @@
 
 def kernel(
     owners, gradient_ref, prior_hbm, mixed_ref, statistic_ref, graft_ref, held, keep_gram, keep_matrix, keep_factor,
-    keep_square, prior_ref, local_sem, prior_sem, send_sem, recv_sem,
+    keep_square, prior_ref, local_sem, prior_sem, send_sem, recv_sem, credit,
 ):
     me = lax.axis_index("expert")
     experts = owners
     slab_rows, width = held.shape[1:]
     rows = experts * slab_rows
     barrier = pltpu.get_barrier_semaphore()
-    for step in range(1, owners):
-        pl.semaphore_signal(
-            barrier, inc=1, device_id={"expert": lax.rem(me + step, owners)}, device_id_type=pl.DeviceIdType.MESH
-        )
+
+    def signal(semaphore, device):
+        pl.semaphore_signal(semaphore, inc=1, device_id={"expert": device}, device_id_type=pl.DeviceIdType.MESH)
+
+    for peer in range(1, owners):
+
+        @pl.when(peer > me)
+        def _():
+            signal(barrier, peer)
+
     local = pltpu.make_async_copy(gradient_ref.at[0], held.at[me], local_sem)
     local.start()
     prior_copy = pltpu.make_async_copy(prior_hbm, prior_ref, prior_sem)
     prior_copy.start()
-    pl.semaphore_wait(barrier, owners - 1)
-    made = []
-    for step in range(1, owners):
-        copy = pltpu.make_async_remote_copy(
+
+    @pl.when(me > 0)
+    def _():
+        pl.semaphore_wait(barrier, me)
+
+    def send(owner, peer):
+        return pltpu.make_async_remote_copy(
             src_ref=gradient_ref.at[0],
-            dst_ref=held.at[me],
-            send_sem=send_sem.at[step],
-            recv_sem=recv_sem.at[step],
-            device_id={"expert": lax.rem(me + step, owners)},
+            dst_ref=held.at[owner],
+            send_sem=send_sem.at[peer],
+            recv_sem=recv_sem.at[owner],
+            device_id={"expert": peer},
             device_id_type=pl.DeviceIdType.MESH,
         )
-        copy.start()
-        made.append(copy)
+
+    for peer in range(owners - 1):
+
+        @pl.when(peer < me)
+        def _():
+            signal(credit.at[me], peer)
+            send(me, peer).start()
+
+    for peer in range(1, owners):
+
+        @pl.when(peer > me)
+        def _():
+            pl.semaphore_wait(credit.at[peer], 1)
+            send(me, peer).start()
 
     tile = (experts, LANES)
     row = lax.broadcasted_iota(jnp.int32, tile, 0)
@@ -139,8 +160,12 @@
     prior_wide = [jnp.broadcast_to(prior_ref[:, k : k + 1], tile) for k in range(experts)]
 
     local.wait()
-    for copy in made:
-        copy.wait()
+    for peer in range(owners):
+
+        @pl.when(peer != me)
+        def _():
+            send(peer, peer).wait_recv()
+            send(me, peer).wait_send()
 
     flat = held[...].reshape(rows, width)
     full = lax.dot_general(flat, flat, (((1,), (1,)), ((), ())), preferred_element_type=jnp.float32)
@@ -232,6 +257,7 @@
             pltpu.SemaphoreType.DMA,
             pltpu.SemaphoreType.DMA((owners,)),
             pltpu.SemaphoreType.DMA((owners,)),
+            pltpu.SemaphoreType.REGULAR((owners,)),
         ],
         compiler_params=pltpu.CompilerParams(
             collective_id=0, has_side_effects=True, vmem_limit_bytes=KERNEL_VMEM

time: 15.7 us -> 15 us (0.955)
  the two profiles are of different devices: /device:TPU:13 before, /device:TPU:0 now
where the time goes in v6:
time: 15 us; the launch traced here: 14.9 us
  Pallas kernels  14.2 us (95%)
  between operations  0.64 us (4%)
    pallas_call x1, Pallas kernels, gathered_body(): pl.pallas_call(functools.partial(kernel, owners), out_shape=(pltpu.VMEM((...  13.6 us
    pallas_call x1, Pallas kernels, gathered_body(): pl.pallas_call(finish, out_shape=(jax.ShapeDtypeStruct(gradient.shape, jn...  0.64 us

profile of v6, /device:TPU:0, one launch (start us, length us, event | category | flops | bytes accessed | tf_op | source)
XLA Modules:
  0.0 14.9 jit_solution(4588002789462194590)
XLA Ops:
  0.6 13.6 %shampoo_step.1 = (bf16[16,1536]{1,0:T(8,128)(2,1)S(1)}, f32[8,128]{1,0:T(8,128)S(1)}, f32[8,128]{1,0:T(8,128)S(1)}) custom-call(bf16[1,16,1536]{2,1,0:T(8,128)(2,1)} %gradient_ref.1, f32[8,8]{1,0:T(8,128)} %prior_hbm.1), custom_call_target="tpu_custom_call" | custom-call | tf_op jit(solution)/shard_map/shampoo_step/pallas_call | solution.py:240
  14.2 0.6 %finish.1 = (bf16[1,16,1536]{2,1,0:T(8,128)(2,1)}, f32[8,8]{1,0:T(8,128)}) custom-call(bf16[16,1536]{1,0:T(8,128)(2,1)S(1)} %get-tuple-element.5.mixed_ref, f32[8,128]{1,0:T(8,128)S(1)} %get-tuple-element.6.wide_ref, f32[8,128]{1,0:T(8,128)S(1)} %get-tuple-element.7.graft_ref), custom_call_target="tpu_custom_call" | custom-call | tf_op jit(solution)/shard_map/finish/pallas_call | solution.py:267
